TPU v7x, 256 devices: a whole 4x4x8 slice. The times are simulated.
256 devices in a mesh: ex: 32 (over z, y_lo, core), tok: 8 (over y_hi, x).
Axes of the slice: x: 4, y: 4 (y_hi: 2, y_lo: 2; y = y_hi * 2 + y_lo), z: 8, core: 2. Of those that a mesh axis runs over, the one named last changes fastest.
Arguments:
- activations: bfloat16 [8192, 32, 4096], P(('ex', 'tok')), may hold values from -6 to 6
- out_grads: bfloat16 [8192, 32, 2, 1024], P(('ex', 'tok')), may hold values from -6 to 6
- block_len: int32 [8192], P(('ex', 'tok')), may hold values from 1 to 32
- block_dest: int32 [8192, 1], P(('ex', 'tok')), may hold values from 0 to 31; in each aligned block of 32 rows (0 to 31, 32 to 63, ...) at most 2 rows name the same one
- block_slot: int32 [8192], P(('ex', 'tok')), may hold values from 0 to 3
- in_proj: bfloat16 [4096, 128], replicated, may hold values from -0.09375 to 0.09375
- out_proj: bfloat16 [2, 1024, 64], replicated, may hold values from -0.1875 to 0.1875
- query_grads: float32 [64, 8192], P('ex'), may hold values from -6 to 6
- precond: float32 [2, 2, 64, 64], replicated, may hold values from -2 to 2, as said below
Outputs:
- scores: float32 [64, 128], P('tok', 'ex')
Inputs may be any that keep to these rules, and one draw needn't show every extreme that they name: `block_dest`: among the 32 blocks of one device no index of ex is named more than 2 times, a bound that some device reaches; every index of ex is named by some block of the whole array. `precond`: entries of order one or less.
All inputs are finite; a program needn't handle non-finite values.
Results may differ from a plain program's by a relative error of at most 0.0003.
Values sent between devices are 32-bit elements; how exact they have to be, the bound alone decides.
A program may use at most 64 MiB of HBM per device.

v0:
```python
import jax
import jax.numpy as jnp
from jax import lax
from jax.sharding import PartitionSpec as P

R = 64
BLK = 32
EX_DEV = 4
F = 8192


highest = lax.Precision.HIGHEST


def on_device(
    activations,
    out_grads,
    block_len,
    block_dest,
    block_slot,
    in_proj,
    out_proj,
    query_grads,
    precond,
):
    block_count = activations.shape[0]
    block_size = activations.shape[1]
    ex_count = lax.axis_size("ex")
    proj_in = jnp.dot(
        activations.reshape(block_count * block_size, -1),
        in_proj,
        preferred_element_type=jnp.float32,
    )
    proj_in = proj_in.reshape(block_count, block_size, 2, R)
    proj_out = jnp.einsum("btlk,lkr->btlr", out_grads, out_proj, preferred_element_type=jnp.float32)
    position = lax.broadcasted_iota(jnp.int32, (block_count, block_size), 1)
    live_mask = (position < block_len[:, None]).astype(jnp.float32)
    proj_out = proj_out * live_mask[:, :, None, None]
    partial_value = jnp.einsum("btlo,btli->bloi", proj_out, proj_in, precision=highest).reshape(
        block_count, F
    )
    target = block_dest[:, 0]
    example = target * EX_DEV + block_slot
    by_example = (
        example[:, None] == jnp.arange(ex_count * EX_DEV, dtype=jnp.int32)[None, :]
    ).astype(jnp.float32)
    table = jnp.dot(by_example.T, partial_value, precision=highest)
    features = lax.psum_scatter(table, "ex", scatter_dimension=0, tiled=True)
    query_count = query_grads.shape[0]
    queries = query_grads.reshape(query_count, 2, R, R)
    left_side = jnp.einsum("lab,qlbc->qlac", precond[:, 0], queries, precision=highest)
    conditioned = jnp.einsum("qlac,lcd->qlad", left_side, precond[:, 1], precision=highest).reshape(
        query_count, F
    )
    score_terms = jnp.dot(
        lax.all_gather(conditioned, "ex", axis=0, tiled=True), features.T, precision=highest
    ) * (1.0 / (R * BLK))
    return lax.psum_scatter(score_terms, "tok", scatter_dimension=0, tiled=True)


def solution(mesh):
    placed = (
        P(("ex", "tok"), None, None),
        P(("ex", "tok"), None, None, None),
        P(("ex", "tok")),
        P(("ex", "tok"), None),
        P(("ex", "tok")),
        P(),
        P(),
        P("ex", None),
        P(),
    )
    return jax.shard_map(
        on_device, mesh=mesh, in_specs=placed, out_specs=P("tok", "ex"), check_vma=False
    )
```

profile of v0, /device:TPU:1, one launch (start us, length us, event | category | flops | bytes accessed | tf_op | source)
XLA Modules:
  0.0 351.3 jit_solution(176973868079033243)
XLA Ops:
  6.5 0.0 copy-start
  6.5 0.0 all-gather.3.cloned.1.call-start
  6.5 1.0 reshape.37
  7.6 1.2 convolution_bitcast_fusion.1
  8.8 1.2 convolution_bitcast_fusion
  10.0 0.7 reshape.40
  10.8 0.0 all-gather.3.cloned.1.call-update
  10.8 0.0 all-reduce.4.cloned.1.call-start
  10.9 1.5 copy.20
  12.3 0.7 fusion.18
  13.1 0.0 copy-done
  13.1 3.4 fusion.7
  16.5 4.9 %fusion = f32[32,32,2,64]{3,1,2,0:T(8,128)S(1)} fusion(bf16[2,64,4096,1]{2,1,0,3:T(8,128)(2,1)S(1)} %bitcast.51, bf16[32,32,4096]{2,1,0:T(8,128)(2,1)} %param.9), kind=kOutput, calls=%fused_computation | convolution fusion | flops 1073741824 | bytes 9961472 | tf_op jit(solution)/shard_map/dot_general | solution.py:29
  21.4 0.0 copy-start.1
  21.4 0.0 copy-start.2
  21.4 3.7 %fusion.21 = f32[32,2,64,64]{3,2,1,0:T(8,128)S(1)} fusion(f32[32,32,2,64]{3,1,2,0:T(8,128)S(1)} %fusion.7, f32[32,32,2,64]{3,1,2,0:T(8,128)S(1)} %fusion), kind=kOutput, calls=%fused_computation.24 | convolution fusion | flops 100663296 | bytes 2097152 | tf_op jit(solution)/shard_map/btlo,btli->bloi/dot_general | solution.py:39
  25.2 0.7 reshape.39
  25.8 0.0 copy-done.1
  25.8 0.0 copy-done.2
  25.8 0.0 copy-start.4
  25.8 0.0 copy-start.3
  25.9 3.9 %fusion.17 = f32[128,8192]{1,0:T(8,128)} fusion(f32[32,8192]{1,0:T(8,128)S(1)} %reshape.39, s32[32]{0:T(128)S(1)} %bitcast_add_fusion), kind=kOutput, calls=%fused_computation.18 | convolution fusion | flops 402657280 | bytes 5243008 | tf_op jit(solution)/shard_map/dot_general | solution.py:47
  29.7 0.0 all-reduce.4.cloned.1.call-update
  29.8 0.0 copy-done.4
  29.8 0.6 dynamic-slice
  30.4 0.0 copy-done.3
  30.4 0.6 dynamic-slice.2
  32.1 47.5 %all-gather.3.cloned.1.call-done = f32[32,2,8192]{2,1,0:T(2,128)} async-done(((f32[1,2,8192]{2,1,0:T(2,128)}), f32[32,2,8192]{2,1,0:T(2,128)}) %all-gather.3.cloned.1.call-update) | async-done | bytes 2097168 | tf_op jit(solution)/shard_map/all_gather | solution.py:56
  79.6 2.7 reshape.41
  82.3 239.6 %all-reduce.4.cloned.1.call-done = f32[128,8192]{1,0:T(8,128)} async-done(((f32[128,8192]{1,0:T(8,128)}), f32[128,8192]{1,0:T(8,128)}) %all-reduce.4.cloned.1.call-update) | async-done | bytes 4194320
  322.0 2.7 convolution_multiply_fusion
  324.7 19.1 %all-reduce.1 = f32[64,4]{0,1:T(4,128)S(1)} all-reduce(f32[64,4]{0,1:T(4,128)S(1)} %convolution_multiply_fusion), channel_id=3, replica_groups=mesh['ex'=32,'tok'=8] {'tok'}, use_global_device_ids=true, to_apply=%region_1.0.clone | all-reduce | flops 256 | bytes 2048
  343.8 0.7 constant_dynamic-slice_fusion
  (2 shorter events, 0.0 us)
Async XLA Ops:
  6.5 6.5 %copy-start = (bf16[2,1024,64]{1,2,0:T(8,128)(2,1)S(1)}, bf16[2,1024,64]{1,2,0:T(8,128)(2,1)}, u32[]{:S(2)}) copy-start(bf16[2,1024,64]{1,2,0:T(8,128)(2,1)} %param.15) | copy-start | bytes 786436
  6.5 73.1 %all-gather.3.cloned.1.call-start = ((), (), s32[]{:S(2)}) async-start(), calls=%async_computation | async-start | bytes 2162688 | tf_op jit(solution)/shard_map/all_gather | solution.py:56
  10.8 311.2 %all-reduce.4.cloned.1.call-start = ((), (), s32[]{:S(2)}) async-start(), calls=%async_computation.1 | async-start | bytes 8388608
  21.4 4.4 %copy-start.1 = (s32[32]{0:T(128)S(1)}, s32[32]{0:T(128)}, u32[]{:S(2)}) copy-start(s32[32]{0:T(128)} %param.13) | copy-start | bytes 388
  21.4 4.4 %copy-start.2 = (s32[32,1]{0,1:T(1,128)S(1)}, s32[32,1]{0,1:T(1,128)}, u32[]{:S(2)}) copy-start(s32[32,1]{0,1:T(1,128)} %param.12) | copy-start | bytes 388
  25.8 3.9 %copy-start.4 = (u32[256]{0:T(256)S(1)}, u32[256]{0:T(256)}, u32[]{:S(2)}) copy-start(u32[256]{0:T(256)} %constant.12) | copy-start | bytes 3076
  25.8 4.5 %copy-start.3 = (u32[256]{0:T(256)S(1)}, u32[256]{0:T(256)}, u32[]{:S(2)}) copy-start(u32[256]{0:T(256)} %constant.16) | copy-start | bytes 3076
Sparse Core Ops, SparseCore 0:
  10.9 68.6 all-gather.2
  82.3 239.6 all-reduce.3
where the time goes:
time: 354 us; the launch traced here: 351 us
  waiting for transfers between devices  287 us (81%)
  matrix products  21 us (6%)
  blocking collectives  19.1 us (5%)
  between operations  14.7 us (4%)
  local copies, waits for them, and re-layouts  8.42 us (2%)
    unnamed x3, waiting for transfers between devices  240 us
    all_gather x1, waiting for transfers between devices, on_device(): lax.all_gather(conditioned, 'ex', axis=0, tiled=True)  47.5 us
    unnamed x1, blocking collectives  19.1 us
  transfers between devices with their start and end apart: 2, of which 2 were waited for; matrix products, arithmetic and copies ran while one was open for 6% of the time, Pallas kernels for 0%

commit v1 on v0

v1 whole, which is shorter than its diff:
```python
import jax
import jax.numpy as jnp
from jax import lax
from jax.experimental import pallas as pl
from jax.experimental.pallas import tpu as pltpu
from jax.sharding import PartitionSpec as P

f32 = jnp.float32
bf16 = jnp.bfloat16
NZ = 8
NB = 32
BLK = 32
ROWS = NB * BLK
D = 4096
KV = 1024
NCH = 8
CB = NB // NCH
CR = CB * BLK
MESH = pl.DeviceIdType.MESH


def split(x):
    hi = x.astype(bf16)
    return hi, (x - hi.astype(f32)).astype(bf16)


def dot(a, b, ca, cb, precision=None):
    return lax.dot_general(
        a, b, (((ca,), (cb,)), ((), ())), preferred_element_type=f32, precision=precision
    )


def body(
    act, grads, lens, dest, slot, win_h, wout_h, pre_h, q_h, out,
    abuf, gbuf, rbuf, G, qs, win, wout, pre, m0s, m1s, sbuf, r1, r2,
    csem, wsem, zsend, zrecv, ysend, yrecv, bsend, brecv, s1, v1, s2, v2,
):
    ex = lax.axis_index("ex")
    tok = lax.axis_index("tok")
    z, ylo, core = ex // 4, (ex // 2) % 2, ex % 2
    yhi, x = tok // 4, tok % 4
    y = yhi * 2 + ylo

    def block(zb, yl, c):
        return ((zb + 2 * NZ) % NZ * 2 + yl) * 2 + c

    def rows(eb, h):
        return qs.at[pl.ds(pl.multiple_of((eb * 2 + h) * 64, 64), 64)]

    def yneighbour(step):
        yn = (y + step + 4) % 4
        return (z * 4 + (yn % 2) * 2 + core, (yn // 2) * 4 + x)

    sibling = (z * 4 + ylo * 2 + (1 - core), tok)

    def zneighbour(step):
        return (((z + step + NZ) % NZ) * 4 + ylo * 2 + core, tok)

    plane = ((ylo * 2 + core) * 8) + tok

    def plane_peer(i):
        p = (plane + i) % 32
        return (z * 4 + p // 8, p % 8)

    def acopy(i):
        return pltpu.make_async_copy(act.at[pl.ds(i * CR, CR)], abuf.at[pl.ds(i * CR, CR)], csem.at[0, i])

    def gcopy(i):
        return pltpu.make_async_copy(grads.at[pl.ds(i * CR, CR)], gbuf.at[pl.ds(i * CR, CR)], csem.at[1, i])

    qcopies = [
        pltpu.make_async_copy(q_h.at[:, j, :], rows(ex, j), wsem.at[j]) for j in range(2)
    ]
    wcopies = [
        pltpu.make_async_copy(s, d, wsem.at[2 + n])
        for n, (s, d) in enumerate(((win_h, win), (wout_h, wout), (pre_h, pre)))
    ]
    for c in qcopies:
        c.start()
    for c in reversed(wcopies):
        c.start()
    for i in range(NCH):
        acopy(i).start()
        gcopy(i).start()

    barrier = pltpu.get_barrier_semaphore()
    for i in range(1, 32):
        pl.semaphore_signal(barrier, inc=1, device_id=plane_peer(i), device_id_type=MESH)
    for i in range(1, NZ):
        pl.semaphore_signal(barrier, inc=1, device_id=zneighbour(i), device_id_type=MESH)

    def remote(src, dst, ss, rs, dev):
        return pltpu.make_async_remote_copy(
            src_ref=src, dst_ref=dst, send_sem=ss, recv_sem=rs, device_id=dev, device_id_type=MESH
        )

    def zcopy(s, d, h):
        r = rows(block(z - (1 - 2 * d) * s, ylo, core), h)
        return remote(r, r, zsend, zrecv.at[s, d, h], zneighbour(1 - 2 * d))

    def zarrival(s, d, h):
        r = rows(block(z - (1 - 2 * d) * s, ylo, core), h)
        return remote(r, r, zsend, zrecv.at[s - 1, d, h], zneighbour(1 - 2 * d))

    def offset(n):
        s, d = (n + 1) // 2, (n + 1) % 2
        return -(1 - 2 * d) * s

    def ycopy(n, h):
        r = rows(block(z + offset(n), ylo, core), h)
        return remote(r, r, ysend, yrecv.at[n, h], yneighbour(1 - 2 * h))

    def yarrival(n, h):
        r = rows(block(z + offset(n), 1 - ylo, core), h)
        return remote(r, r, ysend, yrecv.at[n, h], yneighbour(1 - 2 * h))

    def bcopy(n, o, h):
        r = rows(block(z + offset(n), ylo if o == 0 else 1 - ylo, core), h)
        return remote(r, r, bsend, brecv, sibling)

    def own():
        for h in range(2):
            qcopies[h].wait()
        pl.semaphore_wait(barrier, 38)
        for h in range(2):
            zcopy(0, 0, h).start()
            zcopy(0, 1, h).start()
            ycopy(0, h).start()
            bcopy(0, 0, h).start()

    def ring(s):
        for h in range(2):
            for d in range(2):
                n = 2 * s - 1 + d
                zarrival(s, d, h).wait_recv()
                if s < 3 or h == d:
                    zcopy(s, d, h).start()
                ycopy(n, h).start()
                bcopy(n, 0, h).start()

    def ring_last():
        for d in range(2):
            zarrival(4, d, d).wait_recv()
            ycopy(7, d).start()
            bcopy(7, 0, d).start()

    def across(ns):
        for n in ns:
            for h in range(2):
                yarrival(n, h).wait_recv()
                bcopy(n, 1, h).start()

    def factors():
        lane = lax.broadcasted_iota(jnp.int32, (64, 64), 1)
        row = lax.broadcasted_iota(jnp.int32, (64, 64), 0)
        order = ((row // 2 + (row % 2) * 32) == lane).astype(bf16)
        same = (row == lane).astype(bf16)
        zero = jnp.zeros((64, 64), bf16)
        for l in range(2):
            hi, lo = split(pre[l, 0])
            hi, lo = (dot(v, order, 1, 0).astype(bf16) for v in (hi, lo))
            hi, lo = (jnp.concatenate([v, zero] if l == 0 else [zero, v], axis=1) for v in (hi, lo))
            for n, v in enumerate((hi, hi, lo)):
                m0s[pl.ds(n * 128 + l * 64, 64)] = v
            hi, lo = split(pre[l, 1])
            hi, lo = (dot(same, v, 1, 1).astype(bf16) for v in (hi, lo))
            hi, lo = (
                jnp.concatenate([v, v, zero, zero] if l == 0 else [zero, zero, v, v], axis=1)
                for v in (hi, lo)
            )
            for n, v in enumerate((hi, hi, lo)):
                m1s[pl.ds(n * 128 + l * 64, 64)] = v

    def chunk(i, carry):
        lanes = lax.broadcasted_iota(jnp.int32, (CR, 128), 1)
        lane32 = lax.broadcasted_iota(jnp.int32, (32, 128), 1)
        t32 = lax.broadcasted_iota(jnp.int32, (32, 128), 0)
        r0 = pl.multiple_of(i * CR, CR)
        acopy(i).wait()
        pi = dot(abuf[pl.ds(r0, CR)], win[...], 1, 0)
        gcopy(i).wait()
        rbuf[...] = dot(gbuf[pl.ds(r0, CR)].reshape(2 * CR, KV), wout[...], 1, 1)
        po = jnp.where(lanes < 64, rbuf[pl.ds(0, CR, stride=2)], rbuf[pl.ds(1, CR, stride=2)])
        po = jnp.concatenate(
            [jnp.where(t32 < lens[i * CB + b], po[b * 32 : (b + 1) * 32], 0.0) for b in range(CB)],
            axis=0,
        )
        hi, lo = split(po)
        oh, ol = split(dot(jnp.concatenate([hi, lo, hi], axis=1), m0s[...], 1, 0))
        hi, lo = split(pi)
        ih, il = split(dot(jnp.concatenate([hi, lo, hi], axis=1), m1s[...], 1, 0))
        for b in range(CB):
            s = slice(b * 32, (b + 1) * 32)
            H = dot(
                jnp.concatenate([oh[s], oh[s], ol[s]], axis=0),
                jnp.concatenate([ih[s], il[s], ih[s]], axis=0),
                0,
                0,
            )
            k0 = pl.multiple_of((i * CB + b) * 64, 64)
            G[pl.ds(k0, 32)] = jnp.where(lane32 < 64, H[0:32, 0:128], H[32:64, 0:128])
            G[pl.ds(k0 + 32, 32)] = jnp.where(lane32 < 64, H[64:96, 128:256], H[96:128, 128:256])
        return carry

    def chunks(a, b):
        lax.fori_loop(a, b, chunk, 0)

    wcopies[2].wait()
    factors()
    wcopies[1].wait()
    wcopies[0].wait()
    chunks(0, 1)
    own()
    chunks(1, 2)
    ring(1)
    chunks(2, 3)
    ring(2)
    across([0])
    chunks(3, 4)
    ring(3)
    across([1, 2])
    chunks(4, 6)
    ring_last()
    across([3, 4])
    chunks(6, 8)
    across([5, 6, 7])
    whole = qs.at[pl.ds(0, 32 * 64)]
    remote(whole, whole, bsend, brecv, sibling).wait_recv()

    def score(c, acc):
        gh, gl = split(G[pl.ds(c, 32, stride=64)])
        qh, ql = split(qs[pl.ds(c, 64, stride=64)])
        return acc + dot(jnp.concatenate([qh, ql], axis=0), jnp.concatenate([gh, gl], axis=0), 1, 1)

    acc = lax.fori_loop(0, 64, score, jnp.zeros((128, 64), f32), unroll=8)
    example = jnp.zeros((64, 128), jnp.int32)
    row = lax.broadcasted_iota(jnp.int32, (64, 128), 0) % 32
    lane = lax.broadcasted_iota(jnp.int32, (64, 128), 1)
    for b in range(NB):
        example = jnp.where(row == b, dest[b] * 4 + slot[b], example)
    onehot = (example == lane).astype(f32)
    table = dot(acc, onehot, 1, 0, lax.Precision.HIGHEST)
    sbuf[...] = ((table[0:64] + table[64:128]) * (1.0 / 2048.0)).reshape(8, 8, 128)

    for i in range(1, 32):
        ed, td = plane_peer(i)
        remote(sbuf.at[td], r1.at[plane], s1, v1, (ed, td)).start()
    r1[plane] = sbuf[tok]
    tiles = r1.at[pl.ds(0, 31)]
    remote(tiles, tiles, s1, v1, sibling).wait_recv()
    r2[z] = jnp.sum(r1[...], axis=0)
    for i in range(1, NZ):
        remote(r2.at[z], r2.at[z], s2, v2, zneighbour(i)).start()
    tiles2 = r2.at[pl.ds(0, 7)]
    remote(tiles2, tiles2, s2, v2, sibling).wait_recv()
    total = jnp.sum(r2[...], axis=0)
    pick = (
        lax.broadcasted_iota(jnp.int32, (4, 128), 1)
        == lax.broadcasted_iota(jnp.int32, (4, 128), 0) + ex * 4
    ).astype(f32)
    out[...] = dot(pick, total, 1, 1, lax.Precision.HIGHEST)

    zs = qs.at[pl.ds(0, 14 * 64)]
    remote(zs, zs, zsend, brecv, sibling).wait_send()
    ys = qs.at[pl.ds(0, 16 * 64)]
    remote(ys, ys, ysend, brecv, sibling).wait_send()
    remote(whole, whole, bsend, brecv, sibling).wait_send()
    remote(tiles, tiles, s1, v1, sibling).wait_send()
    remote(tiles2, tiles2, s2, v2, sibling).wait_send()


def on_device(activations, out_grads, block_len, block_dest, block_slot, in_proj, out_proj, query, precond):
    anyspace = pl.BlockSpec(memory_space=pl.ANY)
    smem = pl.BlockSpec(memory_space=pltpu.SMEM)
    vmem = pl.BlockSpec(memory_space=pltpu.VMEM)
    dma = pltpu.SemaphoreType.DMA
    out = pl.pallas_call(
        body,
        out_shape=jax.ShapeDtypeStruct((4, 8), f32),
        in_specs=[anyspace, anyspace, smem, smem, smem, anyspace, anyspace, anyspace, anyspace],
        out_specs=vmem,
        scratch_shapes=[
            pltpu.VMEM((ROWS, D), bf16),
            pltpu.VMEM((ROWS, 2, KV), bf16),
            pltpu.VMEM((2 * CR, 128), f32),
            pltpu.VMEM((NB * 64, 128), f32),
            pltpu.VMEM((64 * 64, 128), f32),
            pltpu.VMEM((D, 128), bf16),
            pltpu.VMEM((128, KV), bf16),
            pltpu.VMEM((2, 2, 64, 64), f32),
            pltpu.VMEM((384, 128), bf16),
            pltpu.VMEM((384, 256), bf16),
            pltpu.VMEM((8, 8, 128), f32),
            pltpu.VMEM((32, 8, 128), f32),
            pltpu.VMEM((NZ, 8, 128), f32),
            dma((2, NCH)),
            dma((5,)),
            dma,
            dma((4, 2, 2)),
            dma,
            dma((NZ, 2)),
            dma,
            dma,
            dma,
            dma,
            dma,
            dma,
        ],
        compiler_params=pltpu.CompilerParams(
            collective_id=0, has_side_effects=True, vmem_limit_bytes=56 << 20
        ),
    )(
        activations.reshape(ROWS, D),
        out_grads.reshape(ROWS, 2, KV),
        block_len,
        block_dest.reshape(NB),
        block_slot,
        in_proj,
        out_proj.transpose(0, 2, 1).reshape(128, KV),
        precond,
        query.reshape(2, 64, 128).transpose(1, 0, 2),
    )
    return out.T


def solution(mesh):
    both = ("ex", "tok")
    placed = (
        P(both, None, None),
        P(both, None, None, None),
        P(both),
        P(both, None),
        P(both),
        P(),
        P(),
        P("ex", None),
        P(),
    )
    return jax.shard_map(
        on_device, mesh=mesh, in_specs=placed, out_specs=P("tok", "ex"), check_vma=False
    )
```

time: 354 us -> 46.6 us (0.13)
  waiting for transfers between devices: 287 us -> 0 us
  Pallas kernels: 0 us -> 45.2 us
  matrix products: 21 us -> 0 us
  blocking collectives: 19.1 us -> 0 us
  between operations: 14.7 us -> 0.01 us
  local copies, waits for them, and re-layouts: 8.42 us -> 1.26 us
    unnamed x3 -> x0, waiting for transfers between devices: 240 us -> none
    all_gather x1 -> x0, waiting for transfers between devices: 47.5 us -> none  [on_device(): lax.all_gather(conditioned, 'ex', axis=0, tiled=True)]
    pallas_call x0 -> x1, Pallas kernels: none -> 45.2 us  [on_device(): pl.pallas_call(body, out_shape=jax.ShapeDtypeStruct((4, 8), f32), in_spec...]
    dot_general x7 -> x0, matrix products: 21 us -> none  [the longest x1 4.87 us: on_device(): jnp.dot(activations.reshape(block_count * block_size, -1), in_proj, prefe...]
    unnamed x1 -> x0, blocking collectives: 19.1 us -> none
    unnamed x16 -> x1, local copies, waits for them, and re-layouts: 6.73 us -> 1.26 us
  transfers between devices with their start and end apart: 2 -> 0, of which waited for: 2 -> 0; matrix products, arithmetic and copies ran while one was open for 6% -> 0% of each run, Pallas kernels for 0% -> 0%
where the time goes in v1:
time: 46.6 us; the launch traced here: 46.5 us
  Pallas kernels  45.2 us (97%)
  local copies, waits for them, and re-layouts  1.26 us (3%)
    pallas_call x1, Pallas kernels, on_device(): pl.pallas_call(body, out_shape=jax.ShapeDtypeStruct((4, 8), f32), in_spec...  45.2 us
    unnamed x1, local copies, waits for them, and re-layouts  1.26 us

profile of v1, /device:TPU:1, one launch (start us, length us, event | category | flops | bytes accessed | tf_op | source)
XLA Modules:
  0.0 46.5 jit_solution(6794274561620355265)
XLA Ops:
  0.0 45.2 %shard_map.91 = f32[4,8]{1,0:T(4,128)} custom-call(bf16[1024,4096]{1,0:T(8,128)(2,1)} %bitcast.10, bf16[1024,2,1024]{2,1,0:T(2,128)(2,1)} %bitcast.11, s32[32]{0:T(128)} %lens.1, s32[32]{0:T(128)} %bitcast.15, s32[32]{0:T(128)} %slot.1, bf16[4096,128]{1,0:T(8,128)(2,1)} %win_h.1, bf16[128,1024]{1,0:T(8,128)(2,1)} %bitcast.12, f32[2,2,64,64]{3,2,1,0:T(8,128)} %pre_h.1, ...), custom_call_target="tpu_custom_call" | custom-call | tf_op jit(solution)/shard_map/pallas_call | solution.py:277
  45.2 1.3 %copy.11 = f32[8,4]{0,1:T(4,128)} copy(f32[8,4]{0,1:T(4,128)} %bitcast.14) | data formatting | bytes 256

commit v2 on v1

v2 whole, which is shorter than its diff:
```python
import jax
import jax.numpy as jnp
from jax import lax
from jax.experimental import pallas as pl
from jax.experimental.pallas import tpu as pltpu
from jax.sharding import PartitionSpec as P

f32 = jnp.float32
bf16 = jnp.bfloat16
NZ = 8
NB = 32
BLK = 32
ROWS = NB * BLK
D = 4096
KV = 1024
NCH = 4
CB = NB // NCH
CR = CB * BLK
MESH = pl.DeviceIdType.MESH


def split(x):
    hi = x.astype(bf16)
    return hi, (x - hi.astype(f32)).astype(bf16)


def dot(a, b, ca, cb, precision=None):
    return lax.dot_general(
        a, b, (((ca,), (cb,)), ((), ())), preferred_element_type=f32, precision=precision
    )


ORDER = (1, -1, 2, -2, 3, -3, 4)


def body(
    act, grads, lens, dest, slot, win_h, wout_h, pre_h, q_h, out,
    abuf, gbuf, rbuf, pbuf, G, qs, win, wout, pre, m0s, m1s, oh, sbuf, r1, r2,
    csem, wsem, zsend, zrecv, xsend, xrecv, gsend, grecv, hsend, hrecv, s1, v1, s2, v2,
):
    ex = lax.axis_index("ex")
    tok = lax.axis_index("tok")
    z, ylo, core = ex // 4, (ex // 2) % 2, ex % 2
    yhi, x = tok // 4, tok % 4
    y = yhi * 2 + ylo
    half = x % 2

    def device(dz, dy, dx):
        yn, xn = (y + dy + 4) % 4, (x + dx + 4) % 4
        return (((z + dz + NZ) % NZ) * 4 + (yn % 2) * 2 + core, (yn // 2) * 4 + xn)

    sibling = (z * 4 + ylo * 2 + (1 - core), tok)

    def rows(dz, yl, j, start=0, size=64):
        m = ((z + dz + NZ) % NZ) * 2 + yl
        return qs.at[pl.ds(pl.multiple_of((m * 2 + j) * 64 + start, 16), size)]

    plane = (ylo * 2 + core) * 8 + tok

    def plane_peer(i):
        p = (plane + i) % 32
        return (z * 4 + p // 8, p % 8)

    def acopy(i):
        return pltpu.make_async_copy(act.at[pl.ds(i * CR, CR)], abuf.at[pl.ds(i * CR, CR)], csem.at[0, i])

    def gcopy(i):
        return pltpu.make_async_copy(grads.at[pl.ds(i * CR, CR)], gbuf.at[pl.ds(i * CR, CR)], csem.at[1, i])

    def remote(src, dst, ss, rs, dev):
        return pltpu.make_async_remote_copy(
            src_ref=src, dst_ref=dst, send_sem=ss, recv_sem=rs, device_id=dev, device_id_type=MESH
        )

    qcopies = [pltpu.make_async_copy(q_h.at[:, j, :], rows(0, ylo, j), wsem.at[j]) for j in range(2)]
    wcopies = [
        pltpu.make_async_copy(s, d, wsem.at[2 + n])
        for n, (s, d) in enumerate(((win_h, win), (wout_h, wout), (pre_h, pre)))
    ]
    for c in qcopies:
        c.start()
    wcopies[2].start()
    wcopies[0].start()
    acopy(0).start()
    wcopies[1].start()
    gcopy(0).start()
    for i in range(1, NCH):
        acopy(i).start()
        gcopy(i).start()

    barrier = pltpu.get_barrier_semaphore()
    for i in range(1, 32):
        pl.semaphore_signal(barrier, inc=1, device_id=plane_peer(i), device_id_type=MESH)
    for i in range(1, NZ):
        pl.semaphore_signal(barrier, inc=1, device_id=device(i, 0, 0), device_id_type=MESH)

    def zcopy(d):
        r = rows(0, ylo, half)
        return remote(r, r, zsend, zrecv.at[d % NZ], device(d, 0, 0))

    def zarrival(d):
        r = rows(-d, ylo, half)
        return remote(r, r, zsend, zrecv.at[d % NZ], device(d, 0, 0))

    def spread(dz, j, start, size, dy, dx):
        r = rows(dz, ylo, j, start, size)
        remote(r, r, xsend, xrecv, device(0, dy, dx)).start()

    def own():
        for c in qcopies:
            c.wait()
        pl.semaphore_wait(barrier, 38)
        for d in ORDER:
            zcopy(d).start()
        for j in range(2):
            spread(0, j, 0, 32, 1, 0)
            spread(0, j, 32, 32, -1, 0)

    def forward(d):
        zarrival(d).wait_recv()
        spread(-d, half, 0, 16, 1, 1)
        spread(-d, half, 16, 16, -1, 1)
        spread(-d, half, 32, 16, 1, -1)
        spread(-d, half, 48, 16, -1, -1)
        spread(-d, half, 0, 32, 0, 1)
        spread(-d, half, 32, 32, 0, -1)
        spread(-d, half, 0, 32, 1, 0)
        spread(-d, half, 32, 32, -1, 0)

    def factors():
        lane = lax.broadcasted_iota(jnp.int32, (64, 64), 1)
        row = lax.broadcasted_iota(jnp.int32, (64, 64), 0)
        order = ((row // 2 + (row % 2) * 32) == lane).astype(bf16)
        same = (row == lane).astype(bf16)
        zero = jnp.zeros((64, 64), bf16)
        for l in range(2):
            hi, lo = split(pre[l, 0])
            hi, lo = (dot(v, order, 1, 0).astype(bf16) for v in (hi, lo))
            hi, lo = (jnp.concatenate([v, zero] if l == 0 else [zero, v], axis=1) for v in (hi, lo))
            for n, v in enumerate((hi, hi, lo)):
                m0s[pl.ds(n * 128 + l * 64, 64)] = v
            hi, lo = split(pre[l, 1])
            hi, lo = (dot(same, v, 1, 1).astype(bf16) for v in (hi, lo))
            hi, lo = (
                jnp.concatenate([v, v, zero, zero] if l == 0 else [zero, zero, v, v], axis=1)
                for v in (hi, lo)
            )
            for n, v in enumerate((hi, hi, lo)):
                m1s[pl.ds(n * 128 + l * 64, 64)] = v

    def examples():
        example = jnp.zeros((NB, 128), jnp.int32)
        row = lax.broadcasted_iota(jnp.int32, (NB, 128), 0)
        lane = lax.broadcasted_iota(jnp.int32, (NB, 128), 1)
        for b in range(NB):
            example = jnp.where(row == b, dest[b] * 4 + slot[b], example)
        oh[pl.ds(0, NB)] = (example == lane).astype(f32)

    def project(i):
        acopy(i).wait()
        pbuf[...] = dot(abuf[pl.ds(i * CR, CR)], win[...], 1, 0)

    def blocks(i):
        lanes = lax.broadcasted_iota(jnp.int32, (CR, 128), 1)
        lane32 = lax.broadcasted_iota(jnp.int32, (32, 128), 1)
        t32 = lax.broadcasted_iota(jnp.int32, (32, 128), 0)
        gcopy(i).wait()
        rbuf[...] = dot(gbuf[pl.ds(i * CR, CR)].reshape(2 * CR, KV), wout[...], 1, 1)
        po = jnp.where(lanes < 64, rbuf[pl.ds(0, CR, stride=2)], rbuf[pl.ds(1, CR, stride=2)])
        po = jnp.concatenate(
            [jnp.where(t32 < lens[i * CB + b], po[b * 32 : (b + 1) * 32], 0.0) for b in range(CB)],
            axis=0,
        )
        hi, lo = split(po)
        oh_, ol = split(dot(jnp.concatenate([hi, lo, hi], axis=1), m0s[...], 1, 0))
        hi, lo = split(pbuf[...])
        ih, il = split(dot(jnp.concatenate([hi, lo, hi], axis=1), m1s[...], 1, 0))
        for b in range(CB):
            s = slice(b * 32, (b + 1) * 32)
            H = dot(
                jnp.concatenate([oh_[s], oh_[s], ol[s]], axis=0),
                jnp.concatenate([ih[s], il[s], ih[s]], axis=0),
                0,
                0,
            )
            k0 = (i * CB + b) * 64
            G[pl.ds(k0, 32)] = jnp.where(lane32 < 64, H[0:32, 0:128], H[32:64, 0:128])
            G[pl.ds(k0 + 32, 32)] = jnp.where(lane32 < 64, H[64:96, 128:256], H[96:128, 128:256])
        size = CB * 64
        remote(G.at[pl.ds(i * size, size)], G.at[pl.ds(NB * 64 + i * size, size)], gsend, grecv, sibling).start()

    own()
    examples()
    remote(oh.at[pl.ds(0, NB)], oh.at[pl.ds(NB, NB)], hsend, hrecv, sibling).start()
    wcopies[2].wait()
    factors()
    wcopies[0].wait()
    project(0)
    wcopies[1].wait()
    blocks(0)
    forward(ORDER[0])
    forward(ORDER[1])
    project(1)
    forward(ORDER[2])
    forward(ORDER[3])
    blocks(1)
    forward(ORDER[4])
    forward(ORDER[5])
    project(2)
    forward(ORDER[6])
    blocks(2)
    project(3)
    blocks(3)
    remote(oh.at[pl.ds(0, NB)], oh.at[pl.ds(NB, NB)], hsend, hrecv, sibling).wait()
    half_g = G.at[pl.ds(0, NB * 64)]
    remote(half_g, half_g, gsend, grecv, sibling).wait_recv()
    spreads = qs.at[pl.ds(0, 1472)]
    remote(spreads, spreads, xsend, xrecv, sibling).wait_recv()

    def score(c, acc):
        gh, gl = split(G[pl.ds(c, 2 * NB, stride=64)])
        qh, ql = split(qs[pl.ds(c, 32, stride=64)])
        return acc + dot(jnp.concatenate([qh, ql], axis=0), jnp.concatenate([gh, gl], axis=0), 1, 1)

    acc = lax.fori_loop(0, 64, score, jnp.zeros((64, 128), f32), unroll=8)
    which = oh[...]
    table = dot(acc, jnp.concatenate([which, which], axis=0), 1, 0, lax.Precision.HIGHEST)
    sbuf[...] = ((table[0:32] + table[32:64]) * (1.0 / 2048.0)).reshape(8, 4, 128)

    for i in range(1, 32):
        ed, td = plane_peer(i)
        remote(sbuf.at[td], r1.at[plane], s1, v1, (ed, td)).start()
    r1[plane] = sbuf[tok]
    tiles = r1.at[pl.ds(0, 31)]
    remote(tiles, tiles, s1, v1, sibling).wait_recv()
    for c in range(2):
        part = jnp.sum(r1[c * 8 : c * 8 + 8], axis=0) + jnp.sum(r1[16 + c * 8 : 24 + c * 8], axis=0)
        r2[z, 2 * c : 2 * c + 2] = part[0:2]
        r2[z, 4 + 2 * c : 6 + 2 * c] = part[2:4]
    for i in range(1, NZ):
        remote(r2.at[z], r2.at[z], s2, v2, device(i, 0, 0)).start()
    tiles2 = r2.at[pl.ds(0, 7)]
    remote(tiles2, tiles2, s2, v2, sibling).wait_recv()
    total = jnp.sum(r2[...], axis=0)
    pick = (
        lax.broadcasted_iota(jnp.int32, (4, 128), 1)
        == lax.broadcasted_iota(jnp.int32, (4, 128), 0) + ex * 4
    ).astype(f32)
    out[...] = dot(pick, total, 1, 1, lax.Precision.HIGHEST)

    zs = qs.at[pl.ds(0, 7 * 64)]
    remote(zs, zs, zsend, xrecv, sibling).wait_send()
    remote(spreads, spreads, xsend, xrecv, sibling).wait_send()
    remote(half_g, half_g, gsend, grecv, sibling).wait_send()
    remote(tiles, tiles, s1, v1, sibling).wait_send()
    remote(tiles2, tiles2, s2, v2, sibling).wait_send()


def on_device(activations, out_grads, block_len, block_dest, block_slot, in_proj, out_proj, query, precond):
    anyspace = pl.BlockSpec(memory_space=pl.ANY)
    smem = pl.BlockSpec(memory_space=pltpu.SMEM)
    vmem = pl.BlockSpec(memory_space=pltpu.VMEM)
    dma = pltpu.SemaphoreType.DMA
    out = pl.pallas_call(
        body,
        out_shape=jax.ShapeDtypeStruct((4, 8), f32),
        in_specs=[anyspace, anyspace, smem, smem, smem, anyspace, anyspace, anyspace, anyspace],
        out_specs=vmem,
        scratch_shapes=[
            pltpu.VMEM((ROWS, D), bf16),
            pltpu.VMEM((ROWS, 2, KV), bf16),
            pltpu.VMEM((2 * CR, 128), f32),
            pltpu.VMEM((CR, 128), f32),
            pltpu.VMEM((2 * NB * 64, 128), f32),
            pltpu.VMEM((32 * 64, 128), f32),
            pltpu.VMEM((D, 128), bf16),
            pltpu.VMEM((128, KV), bf16),
            pltpu.VMEM((2, 2, 64, 64), f32),
            pltpu.VMEM((384, 128), bf16),
            pltpu.VMEM((384, 256), bf16),
            pltpu.VMEM((2 * NB, 128), f32),
            pltpu.VMEM((8, 4, 128), f32),
            pltpu.VMEM((32, 4, 128), f32),
            pltpu.VMEM((NZ, 8, 128), f32),
            dma((2, NCH)),
            dma((5,)),
            dma,
            dma((NZ,)),
            dma,
            dma,
            dma,
            dma,
            dma,
            dma,
            dma,
            dma,
            dma,
            dma,
        ],
        compiler_params=pltpu.CompilerParams(
            collective_id=0, has_side_effects=True, vmem_limit_bytes=56 << 20
        ),
    )(
        activations.reshape(ROWS, D),
        out_grads.reshape(ROWS, 2, KV),
        block_len,
        block_dest.reshape(NB),
        block_slot,
        in_proj,
        out_proj.transpose(0, 2, 1).reshape(128, KV),
        precond,
        query.reshape(2, 64, 128).transpose(1, 0, 2),
    )
    return out.T


def solution(mesh):
    both = ("ex", "tok")
    placed = (
        P(both, None, None),
        P(both, None, None, None),
        P(both),
        P(both, None),
        P(both),
        P(),
        P(),
        P("ex", None),
        P(),
    )
    return jax.shard_map(
        on_device, mesh=mesh, in_specs=placed, out_specs=P("tok", "ex"), check_vma=False
    )
```

time: 46.6 us -> 39.5 us (0.85)
  Pallas kernels: 45.2 us -> 38.1 us
    pallas_call x1, Pallas kernels: 45.2 us -> 38.1 us  [on_device(): pl.pallas_call(body, out_shape=jax.ShapeDtypeStruct((4, 8), f32), in_spec...]
where the time goes in v2:
time: 39.5 us; the launch traced here: 39.4 us
  Pallas kernels  38.1 us (96%)
  local copies, waits for them, and re-layouts  1.26 us (3%)
    pallas_call x1, Pallas kernels, on_device(): pl.pallas_call(body, out_shape=jax.ShapeDtypeStruct((4, 8), f32), in_spec...  38.1 us
    unnamed x1, local copies, waits for them, and re-layouts  1.26 us

profile of v2, /device:TPU:1, one launch (start us, length us, event | category | flops | bytes accessed | tf_op | source)
XLA Modules:
  0.0 39.4 jit_solution(16010539284255521184)
XLA Ops:
  0.0 38.1 %shard_map.91 = f32[4,8]{1,0:T(4,128)} custom-call(bf16[1024,4096]{1,0:T(8,128)(2,1)} %bitcast.10, bf16[1024,2,1024]{2,1,0:T(2,128)(2,1)} %bitcast.11, s32[32]{0:T(128)} %lens.1, s32[32]{0:T(128)} %bitcast.15, s32[32]{0:T(128)} %slot.1, bf16[4096,128]{1,0:T(8,128)(2,1)} %win_h.1, bf16[128,1024]{1,0:T(8,128)(2,1)} %bitcast.12, f32[2,2,64,64]{3,2,1,0:T(8,128)} %pre_h.1, ...), custom_call_target="tpu_custom_call" | custom-call | tf_op jit(solution)/shard_map/pallas_call | solution.py:264
  38.1 1.3 %copy.11 = f32[8,4]{0,1:T(4,128)} copy(f32[8,4]{0,1:T(4,128)} %bitcast.14) | data formatting | bytes 256

commit v3 on v2

--- a/solution.py
+++ b/solution.py
@@ -24,6 +24,13 @@
     return hi, (x - hi.astype(f32)).astype(bf16)
 
 
+def terms(x):
+    hi = x.astype(bf16)
+    rest = x - hi.astype(f32)
+    mid = rest.astype(bf16)
+    return jnp.concatenate([hi, mid, (rest - mid.astype(f32)).astype(bf16)], axis=1)
+
+
 def dot(a, b, ca, cb, precision=None):
     return lax.dot_general(
         a, b, (((ca,), (cb,)), ((), ())), preferred_element_type=f32, precision=precision
@@ -31,11 +38,15 @@
 
 
 ORDER = (1, -1, 2, -2, 3, -3, 4)
+PEERS = sorted(
+    [(dy, dx, dc) for dy in (-1, 0, 1, 2) for dx in (-1, 0, 1, 2) for dc in (0, 1)],
+    key=lambda p: -abs(p[0]) - abs(p[1]) - 0.1 * p[2],
+)[:31]
 
 
 def body(
-    act, grads, lens, dest, slot, win_h, wout_h, pre_h, q_h, out,
-    abuf, gbuf, rbuf, pbuf, G, qs, win, wout, pre, m0s, m1s, oh, sbuf, r1, r2,
+    act, grads, lens_h, dest_h, slot_h, win_h, wout_h, pre_h, q_h, out,
+    lens, dest, slot, abuf, gbuf, rbuf, pbuf, G, qs, win, wout, pre, m0s, m1s, gs, oh, sbuf, r1, r2,
     csem, wsem, zsend, zrecv, xsend, xrecv, gsend, grecv, hsend, hrecv, s1, v1, s2, v2,
 ):
     ex = lax.axis_index("ex")
@@ -58,8 +69,9 @@
     plane = (ylo * 2 + core) * 8 + tok
 
     def plane_peer(i):
-        p = (plane + i) % 32
-        return (z * 4 + p // 8, p % 8)
+        dy, dx, dc = PEERS[i]
+        e, t = device(0, dy, dx)
+        return ((e // 2) * 2 + (core + dc) % 2, t)
 
     def acopy(i):
         return pltpu.make_async_copy(act.at[pl.ds(i * CR, CR)], abuf.at[pl.ds(i * CR, CR)], csem.at[0, i])
@@ -75,12 +87,20 @@
     qcopies = [pltpu.make_async_copy(q_h.at[:, j, :], rows(0, ylo, j), wsem.at[j]) for j in range(2)]
     wcopies = [
         pltpu.make_async_copy(s, d, wsem.at[2 + n])
-        for n, (s, d) in enumerate(((win_h, win), (wout_h, wout), (pre_h, pre)))
+        for n, (s, d) in enumerate(
+            ((win_h, win), (wout_h, wout), (pre_h, pre), (lens_h, lens), (dest_h, dest), (slot_h, slot))
+        )
     ]
+    barrier = pltpu.get_barrier_semaphore()
+    for d in reversed(ORDER):
+        pl.semaphore_signal(barrier, inc=1, device_id=device(d, 0, 0), device_id_type=MESH)
+    for i in range(31):
+        pl.semaphore_signal(barrier, inc=1, device_id=plane_peer(i), device_id_type=MESH)
+
     for c in qcopies:
         c.start()
-    wcopies[2].start()
-    wcopies[0].start()
+    for n in (2, 4, 5, 3, 0):
+        wcopies[n].start()
     acopy(0).start()
     wcopies[1].start()
     gcopy(0).start()
@@ -88,15 +108,8 @@
         acopy(i).start()
         gcopy(i).start()
 
-    barrier = pltpu.get_barrier_semaphore()
-    for i in range(1, 32):
-        pl.semaphore_signal(barrier, inc=1, device_id=plane_peer(i), device_id_type=MESH)
-    for i in range(1, NZ):
-        pl.semaphore_signal(barrier, inc=1, device_id=device(i, 0, 0), device_id_type=MESH)
-
     def zcopy(d):
-        r = rows(0, ylo, half)
-        return remote(r, r, zsend, zrecv.at[d % NZ], device(d, 0, 0))
+        return remote(q_h.at[:, half, :], rows(0, ylo, half), zsend, zrecv.at[d % NZ], device(d, 0, 0))
 
     def zarrival(d):
         r = rows(-d, ylo, half)
@@ -107,14 +120,15 @@
         remote(r, r, xsend, xrecv, device(0, dy, dx)).start()
 
     def own():
-        for c in qcopies:
-            c.wait()
         pl.semaphore_wait(barrier, 38)
         for d in ORDER:
             zcopy(d).start()
         for j in range(2):
-            spread(0, j, 0, 32, 1, 0)
-            spread(0, j, 32, 32, -1, 0)
+            for k in range(2):
+                remote(
+                    q_h.at[pl.ds(k * 32, 32), j, :], rows(0, ylo, j, k * 32, 32), xsend, xrecv,
+                    device(0, 1 - 2 * k, 0),
+                ).start()
 
     def forward(d):
         zarrival(d).wait_recv()
@@ -189,45 +203,65 @@
         size = CB * 64
         remote(G.at[pl.ds(i * size, size)], G.at[pl.ds(NB * 64 + i * size, size)], gsend, grecv, sibling).start()
 
-    own()
-    examples()
-    remote(oh.at[pl.ds(0, NB)], oh.at[pl.ds(NB, NB)], hsend, hrecv, sibling).start()
+    def prepare(part):
+        def some(o, carry):
+            for u in range(8):
+                hi, lo = split(G[pl.ds(part * NB * 64 + o * 8 + u, NB, stride=64)])
+                r0 = pl.multiple_of((o * 8 + u) * 128 + part * 64, 64)
+                gs[pl.ds(r0, NB)] = hi
+                gs[pl.ds(r0 + NB, NB)] = lo
+            return carry
+
+        return some
+
+    half_g = G.at[pl.ds(0, NB * 64)]
+    hcopy = remote(oh.at[pl.ds(0, NB)], oh.at[pl.ds(NB, NB)], hsend, hrecv, sibling)
     wcopies[2].wait()
     factors()
+    own()
+    wcopies[4].wait()
+    wcopies[5].wait()
+    examples()
+    hcopy.start()
+    wcopies[3].wait()
     wcopies[0].wait()
     project(0)
     wcopies[1].wait()
     blocks(0)
+    project(1)
+    blocks(1)
     forward(ORDER[0])
     forward(ORDER[1])
-    project(1)
+    project(2)
+    blocks(2)
     forward(ORDER[2])
     forward(ORDER[3])
-    blocks(1)
+    project(3)
+    blocks(3)
     forward(ORDER[4])
     forward(ORDER[5])
-    project(2)
+    lax.fori_loop(0, 8, prepare(0), 0)
     forward(ORDER[6])
-    blocks(2)
-    project(3)
-    blocks(3)
-    remote(oh.at[pl.ds(0, NB)], oh.at[pl.ds(NB, NB)], hsend, hrecv, sibling).wait()
-    half_g = G.at[pl.ds(0, NB * 64)]
+    hcopy.wait()
     remote(half_g, half_g, gsend, grecv, sibling).wait_recv()
+    lax.fori_loop(0, 8, prepare(1), 0)
     spreads = qs.at[pl.ds(0, 1472)]
     remote(spreads, spreads, xsend, xrecv, sibling).wait_recv()
 
-    def score(c, acc):
-        gh, gl = split(G[pl.ds(c, 2 * NB, stride=64)])
-        qh, ql = split(qs[pl.ds(c, 32, stride=64)])
-        return acc + dot(jnp.concatenate([qh, ql], axis=0), jnp.concatenate([gh, gl], axis=0), 1, 1)
-
-    acc = lax.fori_loop(0, 64, score, jnp.zeros((64, 128), f32), unroll=8)
-    which = oh[...]
-    table = dot(acc, jnp.concatenate([which, which], axis=0), 1, 0, lax.Precision.HIGHEST)
+    for c in qcopies:
+        c.wait()
+    left = []
+    right = []
+    for c in range(64):
+        left.append(jnp.concatenate(split(qs[pl.ds(c, 32, stride=64)]), axis=0))
+        right.append(gs[pl.ds(c * 128, 128)])
+    acc = dot(jnp.concatenate(left, axis=1), jnp.concatenate(right, axis=1), 1, 1)
+    which = oh[...].astype(bf16)
+    which = jnp.concatenate([which[:NB]] * 2 + [which[NB:]] * 2, axis=0)
+    table = dot(terms(acc), jnp.concatenate([which] * 3, axis=0), 1, 0)
     sbuf[...] = ((table[0:32] + table[32:64]) * (1.0 / 2048.0)).reshape(8, 4, 128)
 
-    for i in range(1, 32):
+    for i in range(31):
         ed, td = plane_peer(i)
         remote(sbuf.at[td], r1.at[plane], s1, v1, (ed, td)).start()
     r1[plane] = sbuf[tok]
@@ -237,16 +271,16 @@
         part = jnp.sum(r1[c * 8 : c * 8 + 8], axis=0) + jnp.sum(r1[16 + c * 8 : 24 + c * 8], axis=0)
         r2[z, 2 * c : 2 * c + 2] = part[0:2]
         r2[z, 4 + 2 * c : 6 + 2 * c] = part[2:4]
-    for i in range(1, NZ):
-        remote(r2.at[z], r2.at[z], s2, v2, device(i, 0, 0)).start()
+    for d in reversed(ORDER):
+        remote(r2.at[z], r2.at[z], s2, v2, device(d, 0, 0)).start()
     tiles2 = r2.at[pl.ds(0, 7)]
     remote(tiles2, tiles2, s2, v2, sibling).wait_recv()
     total = jnp.sum(r2[...], axis=0)
     pick = (
         lax.broadcasted_iota(jnp.int32, (4, 128), 1)
         == lax.broadcasted_iota(jnp.int32, (4, 128), 0) + ex * 4
-    ).astype(f32)
-    out[...] = dot(pick, total, 1, 1, lax.Precision.HIGHEST)
+    ).astype(bf16)
+    out[...] = dot(jnp.concatenate([pick] * 3, axis=1), terms(total), 1, 1)
 
     zs = qs.at[pl.ds(0, 7 * 64)]
     remote(zs, zs, zsend, xrecv, sibling).wait_send()
@@ -258,15 +292,17 @@
 
 def on_device(activations, out_grads, block_len, block_dest, block_slot, in_proj, out_proj, query, precond):
     anyspace = pl.BlockSpec(memory_space=pl.ANY)
-    smem = pl.BlockSpec(memory_space=pltpu.SMEM)
     vmem = pl.BlockSpec(memory_space=pltpu.VMEM)
     dma = pltpu.SemaphoreType.DMA
     out = pl.pallas_call(
         body,
         out_shape=jax.ShapeDtypeStruct((4, 8), f32),
-        in_specs=[anyspace, anyspace, smem, smem, smem, anyspace, anyspace, anyspace, anyspace],
+        in_specs=[anyspace] * 9,
         out_specs=vmem,
         scratch_shapes=[
+            pltpu.SMEM((NB,), jnp.int32),
+            pltpu.SMEM((NB,), jnp.int32),
+            pltpu.SMEM((NB,), jnp.int32),
             pltpu.VMEM((ROWS, D), bf16),
             pltpu.VMEM((ROWS, 2, KV), bf16),
             pltpu.VMEM((2 * CR, 128), f32),
@@ -278,12 +314,13 @@
             pltpu.VMEM((2, 2, 64, 64), f32),
             pltpu.VMEM((384, 128), bf16),
             pltpu.VMEM((384, 256), bf16),
+            pltpu.VMEM((64 * 128, 128), bf16),
             pltpu.VMEM((2 * NB, 128), f32),
             pltpu.VMEM((8, 4, 128), f32),
             pltpu.VMEM((32, 4, 128), f32),
             pltpu.VMEM((NZ, 8, 128), f32),
             dma((2, NCH)),
-            dma((5,)),
+            dma((8,)),
             dma,
             dma((NZ,)),
             dma,

time: 39.5 us -> 38 us (0.962)
  Pallas kernels: 38.1 us -> 36.7 us
    pallas_call x1, Pallas kernels: 38.1 us -> 36.7 us  [on_device(): pl.pallas_call(body, out_shape=jax.ShapeDtypeStruct((4, 8), f32), in_spec...]
where the time goes in v3:
time: 38 us; the launch traced here: 37.9 us
  Pallas kernels  36.7 us (97%)
  local copies, waits for them, and re-layouts  1.26 us (3%)
    pallas_call x1, Pallas kernels, on_device(): pl.pallas_call(body, out_shape=jax.ShapeDtypeStruct((4, 8), f32), in_spec...  36.7 us
    unnamed x1, local copies, waits for them, and re-layouts  1.26 us

profile of v3, /device:TPU:1, one launch (start us, length us, event | category | flops | bytes accessed | tf_op | source)
XLA Modules:
  0.0 37.9 jit_solution(7663632322662420863)
XLA Ops:
  0.0 36.7 %shard_map.91 = f32[4,8]{1,0:T(4,128)} custom-call(bf16[1024,4096]{1,0:T(8,128)(2,1)} %bitcast.10, bf16[1024,2,1024]{2,1,0:T(2,128)(2,1)} %bitcast.11, s32[32]{0:T(128)} %lens_h.1, s32[32]{0:T(128)} %bitcast.15, s32[32]{0:T(128)} %slot_h.1, bf16[4096,128]{1,0:T(8,128)(2,1)} %win_h.1, bf16[128,1024]{1,0:T(8,128)(2,1)} %bitcast.12, f32[2,2,64,64]{3,2,1,0:T(8,128)} %pre_h.1, ...), custom_call_target="tpu_custom_call" | custom-call | tf_op jit(solution)/shard_map/pallas_call | solution.py:297
  36.7 1.3 %copy.11 = f32[8,4]{0,1:T(4,128)} copy(f32[8,4]{0,1:T(4,128)} %bitcast.14) | data formatting | bytes 256

commit v4 on v3

--- a/solution.py
+++ b/solution.py
@@ -37,7 +37,7 @@
     )
 
 
-ORDER = (1, -1, 2, -2, 3, -3, 4)
+ORDER = (1, -1, 2, -2, 4, 3, -3)
 PEERS = sorted(
     [(dy, dx, dc) for dy in (-1, 0, 1, 2) for dx in (-1, 0, 1, 2) for dc in (0, 1)],
     key=lambda p: -abs(p[0]) - abs(p[1]) - 0.1 * p[2],

time: 38 us -> 37.9 us (level)
  no operation moved by 1% of the time
where the time goes in v4:
time: 37.9 us; the launch traced here: 37.8 us
  Pallas kernels  36.6 us (97%)
  local copies, waits for them, and re-layouts  1.26 us (3%)
    pallas_call x1, Pallas kernels, on_device(): pl.pallas_call(body, out_shape=jax.ShapeDtypeStruct((4, 8), f32), in_spec...  36.6 us
    unnamed x1, local copies, waits for them, and re-layouts  1.26 us

profile of v4, /device:TPU:1, one launch (start us, length us, event | category | flops | bytes accessed | tf_op | source)
XLA Modules:
  0.0 37.8 jit_solution(17597992703820082344)
XLA Ops:
  0.0 36.6 %shard_map.91 = f32[4,8]{1,0:T(4,128)} custom-call(bf16[1024,4096]{1,0:T(8,128)(2,1)} %bitcast.10, bf16[1024,2,1024]{2,1,0:T(2,128)(2,1)} %bitcast.11, s32[32]{0:T(128)} %lens_h.1, s32[32]{0:T(128)} %bitcast.15, s32[32]{0:T(128)} %slot_h.1, bf16[4096,128]{1,0:T(8,128)(2,1)} %win_h.1, bf16[128,1024]{1,0:T(8,128)(2,1)} %bitcast.12, f32[2,2,64,64]{3,2,1,0:T(8,128)} %pre_h.1, ...), custom_call_target="tpu_custom_call" | custom-call | tf_op jit(solution)/shard_map/pallas_call | solution.py:297
  36.6 1.3 %copy.11 = f32[8,4]{0,1:T(4,128)} copy(f32[8,4]{0,1:T(4,128)} %bitcast.14) | data formatting | bytes 256
